TPU v7x, 32 devices: a whole 2x2x4 slice. The times are simulated.
32 devices in a mesh: slab: 2 (over y), seq: 4 (over z), head: 4 (over x, core).
Axes of the slice: x: 2, y: 2, z: 4, core: 2. Of those that a mesh axis runs over, the one named last changes fastest.
Arguments:
- values_first: bfloat16 [4, 1024, 1024], P('slab', 'seq', 'head'), parts along dimension 0, may hold values from -6 to 6
- keys_first: bfloat16 [4, 1024, 1024], P('slab', 'seq', 'head'), parts along dimension 0, may hold values from -0.5 to 0.5
- queries_first: bfloat16 [4, 1024, 1024], P('slab', 'seq', 'head'), parts along dimension 0, may hold values from -0.5 to 0.5
- steps_first: float32 [4, 8, 1024], P('slab', 'head', 'seq'), parts along dimension 0, may hold values from 0 to 0.35
- rates_first: float32 [8], P('head'), may hold values from 1 to 2
- skip_first: float32 [8], P('head'), may hold values from 1 to 4
- gain_first: float32 [1024], P('head'), may hold values from 0.5 to 1.5
- w_values: bfloat16 [8, 128, 128], P('head'), may hold values from -0.5 to 0.5
- w_keys: bfloat16 [8, 128, 256], P('head'), may hold values from -0.046875 to 0.046875
- w_step: bfloat16 [8, 128], P('head'), may hold values from -0.5 to 0.5
- step_bias: float32 [8], P('head'), may hold values from -1 to 1
- rates_second: float32 [8], P('head'), may hold values from 0 to 0.04
- skip_second: float32 [8], P('head'), may hold values from 1 to 4
- gain_second: float32 [1024], P('head'), may hold values from 0.5 to 1.5
Outputs:
- mixed: bfloat16 [4, 1024, 1024], P('slab', 'seq', 'head'), parts along dimension 0
There are 2 independent parts, one for each index of `slab`. A program takes and returns all parts, laid end to end along the dimension named above; an argument that names none is the same for every part. Nothing has to cross between parts.
All inputs are finite; a program needn't handle non-finite values.
Results may differ from a plain program's by a relative error of at most 0.007.
Values may be sent and summed in bfloat16 or wider, within the bound.
A program may use at most 64 MiB of HBM per device.

v0:
```python
import jax
import jax.numpy as jnp
from jax import lax
from jax.sharding import PartitionSpec as P

N = 128
BLOCK = 256
ROWS_DEV = 8


def block_terms(values, keys_in, queries, log_decay, block_len):
    slab_count, length, feat_width = values.shape
    head_count = log_decay.shape[1]
    blocks = length // block_len
    value_blocks = values.reshape(
        slab_count, blocks, block_len, head_count, feat_width // head_count
    )
    key_blocks = keys_in.reshape(
        slab_count, blocks, block_len, head_count, keys_in.shape[2] // head_count
    )
    query_blocks = queries.reshape(
        slab_count, blocks, block_len, head_count, queries.shape[2] // head_count
    )
    running = jnp.cumsum(log_decay.reshape(slab_count, head_count, blocks, block_len), axis=3)
    running_sc = jnp.transpose(running, (0, 2, 1, 3))
    running_pos = jnp.transpose(running, (0, 2, 3, 1))
    scores = jnp.einsum(
        "scihn,scjhn->schij", query_blocks, key_blocks, preferred_element_type=jnp.float32
    )
    row_ids = lax.broadcasted_iota(jnp.int32, (block_len, block_len), 0)
    col_ids = lax.broadcasted_iota(jnp.int32, (block_len, block_len), 1)
    spread = running_sc[..., :, None] - running_sc[..., None, :]
    decays = jnp.exp(jnp.where(row_ids >= col_ids, spread, -jnp.inf))
    mixing = (scores * decays).astype(jnp.bfloat16)
    inner_sum = jnp.einsum(
        "schij,scjhp->scihp", mixing, value_blocks, preferred_element_type=jnp.float32
    )
    to_end = jnp.exp(running_pos[:, :, -1:, :] - running_pos)
    weighted = (key_blocks * to_end[..., None]).astype(jnp.bfloat16)
    local_states = jnp.einsum(
        "scjhn,scjhp->schnp", weighted, value_blocks, preferred_element_type=jnp.float32
    )
    block_logs = running_sc[..., -1]
    return (value_blocks, query_blocks, running_pos, inner_sum, local_states, block_logs)


def entry_states(local_states, block_logs):

    def advance(carried, entry_item):
        update, log_total = entry_item
        return (jnp.exp(log_total)[..., None, None] * carried + update, carried)

    start_state = jnp.zeros(local_states.shape[:1] + local_states.shape[2:], jnp.float32)
    final_state, entries = lax.scan(
        advance, start_state, (jnp.moveaxis(local_states, 1, 0), jnp.moveaxis(block_logs, 1, 0))
    )
    return (final_state, jnp.moveaxis(entries, 0, 1))


def carry_into(final_state, device_log):
    log_totals = lax.all_gather(device_log[None], "seq", axis=0, tiled=True)
    my_index = lax.axis_index("seq")
    ranks_all = lax.iota(jnp.int32, log_totals.shape[0])
    between = jnp.logical_and(
        ranks_all[None, :] > ranks_all[:, None], ranks_all[None, :] < my_index
    ).astype(jnp.float32)
    span_logs = jnp.einsum("dk,ksh->dsh", between, log_totals, precision=lax.Precision.HIGHEST)
    weights = jnp.where((ranks_all < my_index)[:, None, None], jnp.exp(span_logs), 0.0)
    return jnp.sum(
        weights[..., None, None] * lax.all_gather(final_state[None], "seq", axis=0, tiled=True),
        axis=0,
    )


def selective_scan(values, keys_in, queries, log_decay, skip, gain):
    block_len = min(BLOCK, values.shape[1])
    value_blocks, query_blocks, running_pos, inner_sum, local_states, block_logs = block_terms(
        values, keys_in, queries, log_decay, block_len
    )
    final_state, entries = entry_states(local_states, block_logs)
    carried = carry_into(final_state, jnp.sum(block_logs, axis=1))
    before = jnp.cumsum(block_logs, axis=1) - block_logs
    states = (entries + jnp.exp(before)[..., None, None] * carried[:, None]).astype(jnp.bfloat16)
    outer_sum = jnp.einsum(
        "scihn,schnp->scihp", query_blocks, states, preferred_element_type=jnp.float32
    )
    raw_out = (
        inner_sum
        + outer_sum * jnp.exp(running_pos)[..., None]
        + skip[:, None] * value_blocks.astype(jnp.float32)
    )
    scaled = raw_out * lax.rsqrt(jnp.mean(raw_out * raw_out, axis=-1, keepdims=True) + 1e-05)
    normed = (scaled * gain.reshape(skip.shape[0], -1)).astype(jnp.bfloat16)
    return normed.reshape(normed.shape[0], -1, normed.shape[3] * normed.shape[4])


def project_rows(features, w_values, w_keys, w_step):
    slab_count, length, feat_width = features.shape
    head_count = w_values.shape[0]
    split_feat = features.reshape(slab_count, length, head_count, feat_width // head_count)
    values_two = jnp.einsum(
        "slhp,hpk->slhk", split_feat, w_values, preferred_element_type=jnp.float32
    ).astype(jnp.bfloat16)
    keys_two = jnp.einsum(
        "slhp,hpk->slhk", split_feat, w_keys, preferred_element_type=jnp.float32
    ).astype(jnp.bfloat16)
    step_pre = jnp.einsum(
        "slhp,hp->slh", split_feat, w_step, preferred_element_type=jnp.float32
    ).astype(jnp.bfloat16)
    return (values_two, keys_two, step_pre)


def second_scan(values_two, keys_two, step_pre, step_bias, rates_second, skip_second, gain_second):
    slab_count, length, head_count, key_width = keys_two.shape
    step_size = jax.nn.softplus(step_pre.astype(jnp.float32) + step_bias)
    log_decay = -rates_second[None, :, None] * jnp.transpose(step_size, (0, 2, 1))
    return selective_scan(
        values_two.reshape(slab_count, length, -1),
        keys_two[..., :N].reshape(slab_count, length, -1),
        keys_two[..., N:].reshape(slab_count, length, -1),
        log_decay,
        skip_second,
        gain_second,
    )


def columns_from(received):
    slab_count, rows_all, cols_here, last_width = received.shape
    return jnp.transpose(received, (0, 2, 1, 3)).reshape(
        slab_count, cols_here * rows_all, last_width
    )


def local(
    values_first,
    keys_first,
    queries_first,
    steps_first,
    rates_first,
    skip_first,
    gain_first,
    w_values,
    w_keys,
    w_step,
    step_bias,
    rates_second,
    skip_second,
    gain_second,
):
    log_first = -rates_first[None, :, None] * steps_first
    first_out = selective_scan(
        values_first, keys_first, queries_first, log_first, skip_first, gain_first
    )
    slab_count, length, feat_width = first_out.shape
    home_grid = first_out.reshape(slab_count, ROWS_DEV, length // ROWS_DEV, feat_width)
    received = lax.all_to_all(home_grid, "seq", split_axis=2, concat_axis=1, tiled=True)
    rows_all = received.shape[1]
    cols_here = received.shape[2]
    values_two, keys_two, step_pre = project_rows(columns_from(received), w_values, w_keys, w_step)
    result = second_scan(
        values_two, keys_two, step_pre, step_bias, rates_second, skip_second, gain_second
    )
    column_out = result.reshape(received.shape[0], cols_here, rows_all, result.shape[2])
    home_back = lax.all_to_all(column_out, "seq", split_axis=2, concat_axis=1, tiled=True)
    second_home = jnp.transpose(home_back, (0, 2, 1, 3)).reshape(slab_count, length, feat_width)
    return (first_out.astype(jnp.float32) + second_home.astype(jnp.float32)).astype(jnp.bfloat16)


def solution(mesh):
    placed = (
        P("slab", "seq", "head"),
        P("slab", "seq", "head"),
        P("slab", "seq", "head"),
        P("slab", "head", "seq"),
        P("head"),
        P("head"),
        P("head"),
        P("head", None, None),
        P("head", None, None),
        P("head", None),
        P("head"),
        P("head"),
        P("head"),
        P("head"),
    )
    return jax.shard_map(
        local, mesh=mesh, in_specs=placed, out_specs=P("slab", "seq", "head"), check_vma=False
    )
```

profile of v0, /device:TPU:0, one launch (start us, length us, event | category | flops | bytes accessed | tf_op | source)
XLA Modules:
  0.0 120.6 jit_solution(3875513733914524580)
XLA Ops:
  6.5 0.7 neg.13
  7.2 0.8 broadcast_multiply_fusion
  8.0 1.2 %reduce-window.14 = f32[2,2,1,2,128]{4,3,2,1,0:T(2,128)S(1)} reduce-window(f32[2,2,1,2,128]{4,3,2,1,0:T(2,128)S(1)} %bitcast.227, f32[]{:T(128)} %constant.39.clone.1), window={size=1x1x1x1x128 pad=0_0x0_0x0_0x0_0x127_0}, to_apply=%region_0.0 | reduce-window | flops 130048 | bytes 8196 | tf_op jit(solution)/shard_map/reduce-window
  11.0 0.8 copy-done.2
  12.0 0.8 copy-done.1
  12.8 0.9 convolution_add_fusion.1
  13.7 12.7 %all-gather = f32[8,1,2,1]{2,3,1,0:T(1,128)S(1)} all-gather(f32[2,1,2,1]{2,3,1,0:T(1,128)S(1)} %get-tuple-element.31), channel_id=2, replica_groups=mesh['slab'=2,'seq'=4,'head'=4] {'seq'}, dimensions={0}, use_global_device_ids=true | all-gather | bytes 80 | tf_op jit(solution)/shard_map/all_gather | solution.py:61
  27.8 16.8 %all-gather.7.cloned.1.call-done = f32[8,2,128,128]{3,2,1,0:T(8,128)} async-done(((f32[2,2,128,128]{3,2,1,0:T(8,128)}), f32[8,2,128,128]{3,2,1,0:T(8,128)}) %all-gather.7.cloned.1.call-update) | async-done | bytes 1048592 | tf_op jit(solution)/shard_map/all_gather | solution.py:70
  44.6 1.4 %multiply_reduce_fusion.1 = f32[2,2,128,128]{3,2,1,0:T(8,128)S(1)} fusion(f32[4,2,2,128,128]{4,3,2,1,0:T(8,128)} %bitcast.217, f32[4,2,2]{2,1,0:T(2,128)S(1)} %copy.230), kind=kLoop, calls=%fused_computation.21 | loop fusion | flops 458752 | bytes 1310784 | tf_op jit(solution)/shard_map/reduce_sum | solution.py:69
  47.1 0.7 copy-done.5
  48.2 0.9 copy.241
  49.0 3.5 %all-to-all-start = ((bf16[2,8,32,256]{3,1,0,2:T(8,128)(2,1)}), bf16[2,8,32,256]{3,1,0,2:T(8,128)(2,1)S(1)}, u32[]{:S(2)}, u32[]{:S(2)}) async-start(bf16[2,8,32,256]{3,1,0,2:T(8,128)(2,1)} %copy.241), calls=%async_computation | async-start | bytes 524288 | tf_op jit(solution)/shard_map/all_to_all | solution.py:156
  52.7 8.6 %all-to-all-done = bf16[2,8,32,256]{3,1,0,2:T(8,128)(2,1)S(1)} async-done(((bf16[2,8,32,256]{3,1,0,2:T(8,128)(2,1)}), bf16[2,8,32,256]{3,1,0,2:T(8,128)(2,1)S(1)}, u32[]{:S(2)}, u32[]{:S(2)}) %all-to-all-start) | async-done | bytes 262176 | tf_op jit(solution)/shard_map/all_to_all | solution.py:156
  62.9 1.2 %reduce-window.16 = f32[2,2,1,2,128]{4,3,2,1,0:T(2,128)S(1)} reduce-window(f32[2,2,1,2,128]{4,3,2,1,0:T(2,128)S(1)} %reshape.437, f32[]{:T(128)} %constant.39.clone.1), window={size=1x1x1x1x128 pad=0_0x0_0x0_0x0_0x127_0}, to_apply=%region_4.5 | reduce-window | flops 130048 | bytes 8196 | tf_op jit(solution)/shard_map/reduce-window.2
  65.1 0.7 copy-done.4
  67.7 1.2 %convolution_add_fusion = f32[2,2,128,128]{3,2,1,0:T(8,128)} fusion(bf16[2,256,2,128]{1,3,0,2:T(8,128)(2,1)S(1)} %fusion.9, f32[2,2]{1,0:T(2,128)S(1)} %bitcast.237, f32[2,256,2]{1,0,2:T(2,128)S(1)} %copy.260, bf16[2,256,2,256]{3,1,0,2:T(8,128)(2,1)S(1)} %fusion.2), kind=kOutput, calls=%fused_computation.17 | convolution fusion | flops 34013184 | bytes 791552 | tf_op jit(solution)/shard_map/scjhn,scjhp->schnp/dot_general | solution.py:40
  69.0 9.0 %all-gather.2 = f32[8,1,2,1]{2,3,1,0:T(1,128)S(1)} all-gather(f32[2,1,2,1]{2,3,1,0:T(1,128)S(1)} %get-tuple-element.24), channel_id=4, replica_groups=mesh['slab'=2,'seq'=4,'head'=4] {'seq'}, dimensions={0}, use_global_device_ids=true | all-gather | bytes 80 | tf_op jit(solution)/shard_map/all_gather | solution.py:61
  79.4 16.7 %all-gather.9.cloned.1.call-done = f32[8,2,128,128]{3,2,1,0:T(8,128)} async-done(((f32[2,2,128,128]{3,2,1,0:T(8,128)}), f32[8,2,128,128]{3,2,1,0:T(8,128)}) %all-gather.9.cloned.1.call-update) | async-done | bytes 1048592 | tf_op jit(solution)/shard_map/all_gather | solution.py:70
  96.2 1.4 %multiply_reduce_fusion = f32[2,2,128,128]{3,2,1,0:T(8,128)S(1)} fusion(f32[4,2,2,128,128]{4,3,2,1,0:T(8,128)} %bitcast.218, f32[4,2,2]{2,1,0:T(2,128)S(1)} %copy.257), kind=kLoop, calls=%fused_computation.20 | loop fusion | flops 458752 | bytes 1310784 | tf_op jit(solution)/shard_map/reduce_sum | solution.py:69
  98.6 0.7 copy-done.6
  99.8 0.9 copy.270
  100.6 3.4 %all-to-all-start.1 = ((bf16[2,8,32,256]{3,1,0,2:T(8,128)(2,1)}), bf16[2,8,32,256]{3,1,0,2:T(8,128)(2,1)S(1)}, u32[]{:S(2)}, u32[]{:S(2)}) async-start(bf16[2,8,32,256]{3,1,0,2:T(8,128)(2,1)} %copy.270), calls=%async_computation.1 | async-start | bytes 524288 | tf_op jit(solution)/shard_map/all_to_all | solution.py:164
  104.2 8.5 %all-to-all-done.1 = bf16[2,8,32,256]{3,1,0,2:T(8,128)(2,1)S(1)} async-done(((bf16[2,8,32,256]{3,1,0,2:T(8,128)(2,1)}), bf16[2,8,32,256]{3,1,0,2:T(8,128)(2,1)S(1)}, u32[]{:S(2)}, u32[]{:S(2)}) %all-to-all-start.1) | async-done | bytes 262176 | tf_op jit(solution)/shard_map/all_to_all | solution.py:164
  113.0 0.8 fusion.13
  (104 shorter events, 12.5 us)
Async XLA Ops:
  6.5 20.7 %copy-start = (bf16[2,256,256]{2,1,0:T(8,128)(2,1)S(1)}, bf16[2,256,256]{2,1,0:T(8,128)(2,1)}, u32[]{:S(2)}) copy-start(bf16[2,256,256]{2,1,0:T(8,128)(2,1)} %param.16) | copy-start | bytes 786436
  6.5 38.1 %all-gather.7.cloned.1.call-start = ((), (), s32[]{:S(2)}) async-start(), calls=%async_computation.2 | async-start | bytes 1310720 | tf_op jit(solution)/shard_map/all_gather | solution.py:70
  10.9 1.0 copy-start.2
  11.8 0.9 copy-start.1
  46.0 0.7 copy-start.7
  47.0 0.7 copy-start.5
  49.0 3.6 %copy-start.10 = (f32[2]{0:T(128)S(1)}, f32[2]{0:T(128)}, u32[]{:S(2)}) copy-start(f32[2]{0:T(128)} %param.25) | copy-start | bytes 28
  49.0 12.2 %all-to-all-start = ((bf16[2,8,32,256]{3,1,0,2:T(8,128)(2,1)}), bf16[2,8,32,256]{3,1,0,2:T(8,128)(2,1)S(1)}, u32[]{:S(2)}, u32[]{:S(2)}) async-start(bf16[2,8,32,256]{3,1,0,2:T(8,128)(2,1)} %copy.241), calls=%async_computation | async-start | bytes 524288 | tf_op jit(solution)/shard_map/all_to_all | solution.py:156
  52.6 43.6 %all-gather.9.cloned.1.call-start = ((), (), s32[]{:S(2)}) async-start(), calls=%async_computation.3 | async-start | bytes 1310720 | tf_op jit(solution)/shard_map/all_gather | solution.py:70
  61.4 0.7 copy-start.11
  62.1 0.7 copy-start.8
  65.0 0.8 copy-start.4
  65.8 0.9 copy-start.3
  97.6 0.7 copy-start.9
  98.6 0.7 copy-start.6
  100.6 12.0 %all-to-all-start.1 = ((bf16[2,8,32,256]{3,1,0,2:T(8,128)(2,1)}), bf16[2,8,32,256]{3,1,0,2:T(8,128)(2,1)S(1)}, u32[]{:S(2)}, u32[]{:S(2)}) async-start(bf16[2,8,32,256]{3,1,0,2:T(8,128)(2,1)} %copy.270), calls=%async_computation.1 | async-start | bytes 524288 | tf_op jit(solution)/shard_map/all_to_all | solution.py:164
Sparse Core Ops, SparseCore 0:
  13.9 30.6 all-gather.6
  69.1 27.0 all-gather.8
where the time goes:
time: 121 us
  waiting for transfers between devices  50.6 us (42%)
  blocking collectives  21.7 us (18%)
  between operations  13.9 us (11%)
  local copies, waits for them, and re-layouts  12.8 us (11%)
  other arithmetic  9.53 us (8%)
  starting transfers between devices  6.99 us (6%)
  matrix products  5.08 us (4%)
    all_gather x2, waiting for transfers between devices, carry_into(): lax.all_gather(final_state[None], 'seq', axis=0, tiled=True)  33.6 us
    all_gather x2, blocking collectives, carry_into(): log_totals = lax.all_gather(device_log[None], 'seq', axis=0, tiled=True)  21.7 us
    all_to_all x1, waiting for transfers between devices, local(): lax.all_to_all(home_grid, 'seq', split_axis=2, concat_axis=1, tiled=True)  8.57 us
    all_to_all x1, waiting for transfers between devices, local(): lax.all_to_all(column_out, 'seq', split_axis=2, concat_axis=1, tiled=True)  8.49 us
    unnamed x26, local copies, waits for them, and re-layouts  6.96 us
    all_to_all x1, starting transfers between devices, local(): lax.all_to_all(home_grid, 'seq', split_axis=2, concat_axis=1, tiled=True)  3.54 us
    all_to_all x1, starting transfers between devices, local(): lax.all_to_all(column_out, 'seq', split_axis=2, concat_axis=1, tiled=True)  3.41 us
    another operation x6, other arithmetic  3.13 us
  transfers between devices with their start and end apart: 4, of which 4 were waited for; matrix products, arithmetic and copies ran while one was open for 2% of the time, Pallas kernels for 0%

commit v1 on v0

--- a/solution.py
+++ b/solution.py
@@ -1,6 +1,11 @@
+import functools
+import math
+
 import jax
 import jax.numpy as jnp
 from jax import lax
+from jax.experimental import pallas as pl
+from jax.experimental.pallas import tpu as pltpu
 from jax.sharding import PartitionSpec as P
 
 N = 128
@@ -166,7 +171,379 @@
     return (first_out.astype(jnp.float32) + second_home.astype(jnp.float32)).astype(jnp.bfloat16)
 
 
+def cumsum_rows(rows, upper):
+    high = rows.astype(jnp.bfloat16).astype(jnp.float32)
+    rest = rows - high
+    mid = rest.astype(jnp.bfloat16).astype(jnp.float32)
+    low = rest - mid
+    count = rows.shape[0]
+    stacked = jnp.concatenate([high, mid, low, jnp.zeros_like(low)], axis=0).astype(jnp.bfloat16)
+    sums = jnp.dot(stacked, upper, preferred_element_type=jnp.float32)
+    return sums[:count] + sums[count : 2 * count] + sums[2 * count : 3 * count]
+
+
+def dot_nt(left, right):
+    return lax.dot_general(
+        left, right, (((1,), (1,)), ((), ())), preferred_element_type=jnp.float32
+    )
+
+
+def dot_tn(left, right):
+    return lax.dot_general(
+        left, right, (((0,), (0,)), ((), ())), preferred_element_type=jnp.float32
+    )
+
+
+def scan_block(values, keys_in, queries, run_row, state, skip, gain):
+    length, width = values.shape
+    half = length // 2
+    run_col = jnp.transpose(jnp.broadcast_to(run_row, (width, length)))
+    lower = lax.broadcasted_iota(jnp.int32, (half, half), 0) >= lax.broadcasted_iota(
+        jnp.int32, (half, half), 1
+    )
+    reps = half // width
+
+    def decay(rows, columns, masked):
+        left = jnp.concatenate([run_col[rows]] * reps, axis=1) if reps > 1 else run_col[rows]
+        spread = left - run_row[:, columns]
+        return jnp.exp(jnp.where(lower, spread, -jnp.inf) if masked else spread)
+
+    top, bottom = slice(0, half), slice(half, length)
+    scores_top = dot_nt(queries[top], keys_in[top])
+    scores_bottom = dot_nt(queries[bottom], keys_in)
+    mix_top = (scores_top * decay(top, top, True)).astype(jnp.bfloat16)
+    mix_bottom = jnp.concatenate(
+        [
+            (scores_bottom[:, top] * decay(bottom, top, False)).astype(jnp.bfloat16),
+            (scores_bottom[:, bottom] * decay(bottom, bottom, True)).astype(jnp.bfloat16),
+        ],
+        axis=1,
+    )
+    inner = jnp.concatenate(
+        [
+            jnp.dot(mix_top, values[top], preferred_element_type=jnp.float32),
+            jnp.dot(mix_bottom, values, preferred_element_type=jnp.float32),
+        ],
+        axis=0,
+    )
+    raw = inner + skip * values.astype(jnp.float32)
+    if state is not None:
+        outer = jnp.dot(queries, state.astype(jnp.bfloat16), preferred_element_type=jnp.float32)
+        raw = raw + jnp.exp(run_col) * outer
+    mean_sq = jnp.mean(raw * raw, axis=1, keepdims=True)
+    normed = (raw * lax.rsqrt(mean_sq + 1e-05) * gain).astype(jnp.bfloat16)
+    last = run_col[length - 1 : length, :]
+    weighted = (keys_in.astype(jnp.float32) * jnp.exp(last - run_col)).astype(jnp.bfloat16)
+    update = dot_tn(weighted, values)
+    if state is not None:
+        update = update + jnp.exp(last) * state
+    return normed, update
+
+
+def fused_kernel(
+    parts,
+    heads,
+    values,
+    keys_in,
+    queries,
+    steps,
+    w_values,
+    w_keys,
+    w_step,
+    gain_first,
+    gain_second,
+    rates_first,
+    skip_first,
+    step_bias,
+    rates_second,
+    skip_second,
+    out,
+    v_buf,
+    k_buf,
+    q_buf,
+    step_buf,
+    wv_buf,
+    wk_buf,
+    first_buf,
+    turn_buf,
+    send_buf,
+    own_sem,
+    in_send,
+    in_recv,
+    out_own,
+    out_send,
+    out_recv,
+):
+    me = lax.axis_index("seq")
+    length, width = v_buf.shape[1:]
+    rows_all, cols_here = send_buf.shape[1:3]
+    rows_here = rows_all // parts
+    my_slab, my_head = me // heads, lax.rem(me, heads)
+
+    def lanes(head):
+        return pl.ds(pl.multiple_of(head * width, width), width)
+
+    def pieces(owner):
+        slab, head = owner // heads, lax.rem(owner, heads)
+        return (
+            steps.at[slab],
+            keys_in.at[slab, :, lanes(head)],
+            queries.at[slab, :, lanes(head)],
+            values.at[slab, :, lanes(head)],
+        )
+
+    landing = (step_buf, k_buf, q_buf, v_buf)
+
+    barrier = pltpu.get_barrier_semaphore()
+    for hop in range(1, parts):
+        pl.semaphore_signal(
+            barrier,
+            inc=1,
+            device_id={"seq": lax.rem(me + hop, parts)},
+            device_id_type=pl.DeviceIdType.MESH,
+        )
+    own = [
+        pltpu.make_async_copy(src, dst.at[me], own_sem.at[kind])
+        for kind, (src, dst) in enumerate(zip(pieces(me), landing))
+    ]
+    own.append(pltpu.make_async_copy(w_values.at[my_head], wv_buf, own_sem.at[len(landing)]))
+    own.append(pltpu.make_async_copy(w_keys.at[my_head], wk_buf, own_sem.at[len(landing) + 1]))
+    for copy in own:
+        copy.start()
+    pl.semaphore_wait(barrier, parts - 1)
+
+    sends = []
+    for hop in range(1, parts):
+        target = lax.rem(me + hop, parts)
+        for kind, (src, dst) in enumerate(zip(pieces(target), landing)):
+            copy = pltpu.make_async_remote_copy(
+                src_ref=src,
+                dst_ref=dst.at[me],
+                send_sem=in_send.at[kind, hop],
+                recv_sem=in_recv.at[kind, me],
+                device_id={"seq": target},
+                device_id_type=pl.DeviceIdType.MESH,
+            )
+            copy.start()
+            sends.append(copy)
+
+    def await_block(source, kinds):
+        for kind in kinds:
+            src, dst = pieces(me)[kind], landing[kind]
+            pltpu.make_async_remote_copy(
+                src_ref=src,
+                dst_ref=dst.at[source],
+                send_sem=in_send.at[kind, 0],
+                recv_sem=in_recv.at[kind, source],
+                device_id={"seq": source},
+                device_id_type=pl.DeviceIdType.MESH,
+            ).wait_recv()
+
+    upper = jnp.where(
+        lax.broadcasted_iota(jnp.int32, (length, length), 0)
+        <= lax.broadcasted_iota(jnp.int32, (length, length), 1),
+        1.0,
+        0.0,
+    ).astype(jnp.bfloat16)
+
+    def pick(ref, axis_size, select):
+        chosen = select(0)
+        for head in range(1, axis_size):
+            chosen = jnp.where(my_head == head, select(head), chosen)
+        return chosen
+
+    gain_one = pick(gain_first, heads, lambda h: gain_first[:, h * width : (h + 1) * width])
+    gain_two = pick(gain_second, heads, lambda h: gain_second[:, h * width : (h + 1) * width])
+    step_row = pick(w_step, heads, lambda h: w_step[...].astype(jnp.float32)[h : h + 1, :])
+    step_rows = jnp.broadcast_to(step_row, (16, width)).astype(jnp.bfloat16)
+    skip_one, skip_two = skip_first[my_head], skip_second[my_head]
+
+    for copy in own:
+        copy.wait()
+
+    state = None
+    for block in range(parts):
+        @pl.when(me != block)
+        def _():
+            await_block(block, range(len(landing)))
+
+        log_row = -rates_first[my_head] * step_buf[block, pl.ds(my_head, 1), :]
+        run_row = cumsum_rows(jnp.broadcast_to(log_row, (8, length)), upper)[0:1]
+        normed, state = scan_block(
+            v_buf[block], k_buf[block], q_buf[block], run_row, state, skip_one, gain_one
+        )
+        first_buf[pl.ds(block * length, length), :] = normed.astype(jnp.float32)
+
+    state = None
+    for block in range(parts):
+        columns = jnp.concatenate(
+            [
+                first_buf[pl.ds(block * cols_here + col, rows_all, stride=rows_all), :]
+                for col in range(cols_here)
+            ],
+            axis=0,
+        ).astype(jnp.bfloat16)
+        values_two = jnp.dot(
+            columns, wv_buf[...], preferred_element_type=jnp.float32
+        ).astype(jnp.bfloat16)
+        keys_two = jnp.dot(columns, wk_buf[...], preferred_element_type=jnp.float32).astype(
+            jnp.bfloat16
+        )
+        pre = dot_nt(step_rows, columns)[0:8].astype(jnp.bfloat16).astype(jnp.float32)
+        shifted = pre + step_bias[my_head]
+        soft = jnp.maximum(shifted, 0.0) + jnp.log1p(jnp.exp(-jnp.abs(shifted)))
+        run_row = cumsum_rows(-rates_second[my_head] * soft, upper)[0:1]
+        half = keys_two.shape[1] // 2
+        normed, state = scan_block(
+            values_two, keys_two[:, :half], keys_two[:, half:], run_row, state, skip_two, gain_two
+        )
+        turn_buf[block] = normed.astype(jnp.float32)
+        for row in range(rows_all):
+            total = (
+                first_buf[pl.ds(row * rows_all + block * cols_here, cols_here), :]
+                + turn_buf[block, pl.ds(row, cols_here, stride=rows_all), :]
+            )
+            send_buf[block, row] = total.astype(jnp.bfloat16)
+
+        def home(owner):
+            return send_buf.at[block, pl.ds(owner * rows_here, rows_here)]
+
+        def place(owner):
+            slab, head = owner // heads, lax.rem(owner, heads)
+            return out.at[slab, :, pl.ds(block * cols_here, cols_here), lanes(head)]
+
+        for hop in range(1, parts):
+            target = lax.rem(me + hop, parts)
+            copy = pltpu.make_async_remote_copy(
+                src_ref=home(target),
+                dst_ref=place(me),
+                send_sem=out_send.at[block, hop],
+                recv_sem=out_recv.at[block, me],
+                device_id={"seq": target},
+                device_id_type=pl.DeviceIdType.MESH,
+            )
+            copy.start()
+            sends.append(copy)
+        pltpu.make_async_copy(home(me), place(me), out_own.at[block]).start()
+
+    for block in range(parts):
+        def place(owner):
+            slab, head = owner // heads, lax.rem(owner, heads)
+            return out.at[slab, :, pl.ds(block * cols_here, cols_here), lanes(head)]
+
+        mine = send_buf.at[block, pl.ds(me * rows_here, rows_here)]
+        pltpu.make_async_copy(mine, place(me), out_own.at[block]).wait()
+        for hop in range(1, parts):
+            source = lax.rem(me + hop, parts)
+            pltpu.make_async_remote_copy(
+                src_ref=mine,
+                dst_ref=place(source),
+                send_sem=out_send.at[block, 0],
+                recv_sem=out_recv.at[block, source],
+                device_id={"seq": source},
+                device_id_type=pl.DeviceIdType.MESH,
+            ).wait_recv()
+    for copy in sends:
+        copy.wait_send()
+
+
+def local_fused(
+    parts,
+    values_first,
+    keys_first,
+    queries_first,
+    steps_first,
+    rates_first,
+    skip_first,
+    gain_first,
+    w_values,
+    w_keys,
+    w_step,
+    step_bias,
+    rates_second,
+    skip_second,
+    gain_second,
+):
+    slab_count, length, feat_width = values_first.shape
+    heads = rates_first.shape[0]
+    width = feat_width // heads
+    grid_side = math.isqrt(parts * length)
+    rows_here, cols_here = grid_side // parts, length // grid_side
+    anywhere = pl.BlockSpec(memory_space=pl.ANY)
+    vmem = pl.BlockSpec(memory_space=pltpu.VMEM)
+    smem = pl.BlockSpec(memory_space=pltpu.SMEM)
+    dma = pltpu.SemaphoreType.DMA
+    mixed = pl.pallas_call(
+        functools.partial(fused_kernel, parts, heads),
+        out_shape=jax.ShapeDtypeStruct(
+            (slab_count, rows_here, grid_side, feat_width), jnp.bfloat16
+        ),
+        in_specs=[anywhere] * 6 + [vmem] * 3 + [smem] * 5,
+        out_specs=anywhere,
+        scratch_shapes=[
+            pltpu.VMEM((parts, length, width), jnp.bfloat16),
+            pltpu.VMEM((parts, length, width), jnp.bfloat16),
+            pltpu.VMEM((parts, length, width), jnp.bfloat16),
+            pltpu.VMEM((parts, heads, length), jnp.float32),
+            pltpu.VMEM(w_values.shape[1:], jnp.bfloat16),
+            pltpu.VMEM(w_keys.shape[1:], jnp.bfloat16),
+            pltpu.VMEM((parts * length, width), jnp.float32),
+            pltpu.VMEM((parts, length, width), jnp.float32),
+            pltpu.VMEM((parts, grid_side, cols_here, width), jnp.bfloat16),
+            dma((6,)),
+            dma((4, parts)),
+            dma((4, parts)),
+            dma((parts,)),
+            dma((parts, parts)),
+            dma((parts, parts)),
+        ],
+        compiler_params=pltpu.CompilerParams(collective_id=0, has_side_effects=True),
+    )(
+        values_first,
+        keys_first,
+        queries_first,
+        steps_first,
+        w_values,
+        w_keys,
+        w_step,
+        gain_first.reshape(1, -1),
+        gain_second.reshape(1, -1),
+        rates_first,
+        skip_first,
+        step_bias,
+        rates_second,
+        skip_second,
+    )
+    return mixed.reshape(values_first.shape)
+
+
+def fits_fused(parts, args):
+    values, w_values, w_keys = args[0], args[7], args[8]
+    slab_count, length, feat_width = values.shape
+    heads = args[4].shape[0]
+    side = math.isqrt(parts * length)
+    return (
+        slab_count * heads == parts
+        and length <= BLOCK
+        and length % 256 == 0
+        and side * side == parts * length
+        and side % parts == 0
+        and length % side == 0
+        and (length // side) % 8 == 0
+        and feat_width // heads == 128
+        and w_values.shape[1:] == (128, 128)
+        and w_keys.shape[1:] == (128, 256)
+    )
+
+
 def solution(mesh):
+    parts = mesh.shape["seq"]
+
+    def chosen(*args):
+        if fits_fused(parts, args):
+            return local_fused(parts, *args)
+        return local(*args)
+
     placed = (
         P("slab", "seq", "head"),
         P("slab", "seq", "head"),
@@ -184,5 +561,5 @@
         P("head"),
     )
     return jax.shard_map(
-        local, mesh=mesh, in_specs=placed, out_specs=P("slab", "seq", "head"), check_vma=False
-    )
+        chosen, mesh=mesh, in_specs=placed, out_specs=P("slab", "seq", "head"), check_vma=False
+    )

time: 121 us -> 35.8 us (0.30)
  waiting for transfers between devices: 50.6 us -> 0 us
  Pallas kernels: 0 us -> 33.9 us
  blocking collectives: 21.7 us -> 0 us
  between operations: 13.9 us -> 0.01 us
  local copies, waits for them, and re-layouts: 12.8 us -> 1.67 us
  other arithmetic: 9.53 us -> 0 us
  starting transfers between devices: 6.99 us -> 0 us
  matrix products: 5.08 us -> 0 us
    pallas_call x0 -> x1, Pallas kernels: none -> 33.9 us  [local_fused(): pl.pallas_call(functools.partial(fused_kernel, parts, heads), out_shape=j...]
    all_gather x2 -> x0, waiting for transfers between devices: 33.6 us -> none  [carry_into(): lax.all_gather(final_state[None], 'seq', axis=0, tiled=True)]
    all_gather x2 -> x0, blocking collectives: 21.7 us -> none  [carry_into(): log_totals = lax.all_gather(device_log[None], 'seq', axis=0, tiled=True)]
    all_to_all x2 -> x0, waiting for transfers between devices: 17.1 us -> none  [the longest x1 8.57 us: local(): lax.all_to_all(home_grid, 'seq', split_axis=2, concat_axis=1, tiled=True)]
    all_to_all x2 -> x0, starting transfers between devices: 6.95 us -> none  [the longest x1 3.54 us: local(): lax.all_to_all(home_grid, 'seq', split_axis=2, concat_axis=1, tiled=True)]
    unnamed x26 -> x1, local copies, waits for them, and re-layouts: 6.96 us -> 1.67 us
    dot_general x10 -> x0, matrix products: 4.83 us -> none  [the longest x2 2.14 us: block_terms(): jnp.einsum('scjhn,scjhp->schnp', weighted, value_blocks, preferred_elemen...]
    another operation x24 -> x0, local copies, waits for them, and re-layouts: 3.69 us -> none
  transfers between devices with their start and end apart: 4 -> 0, of which waited for: 4 -> 0; matrix products, arithmetic and copies ran while one was open for 2% -> 0% of each run, Pallas kernels for 0% -> 0%
where the time goes in v1:
time: 35.8 us; the launch traced here: 35.6 us
  Pallas kernels  33.9 us (95%)
  local copies, waits for them, and re-layouts  1.67 us (5%)
    pallas_call x1, Pallas kernels, local_fused(): pl.pallas_call(functools.partial(fused_kernel, parts, heads), out_shape=j...  33.9 us
    unnamed x1, local copies, waits for them, and re-layouts  1.67 us

profile of v1, /device:TPU:0, one launch (start us, length us, event | category | flops | bytes accessed | tf_op | source)
XLA Modules:
  0.0 35.6 jit_solution(10539273092166736100)
XLA Ops:
  0.0 33.9 %shard_map.136 = bf16[2,8,32,256]{3,2,1,0:T(8,128)(2,1)} custom-call(bf16[2,256,256]{2,1,0:T(8,128)(2,1)} %values.1, bf16[2,256,256]{2,1,0:T(8,128)(2,1)} %keys_in.1, bf16[2,256,256]{2,1,0:T(8,128)(2,1)} %queries.1, f32[2,2,256]{2,1,0:T(2,128)} %steps.1, bf16[2,128,128]{2,1,0:T(8,128)(2,1)} %w_values.1, bf16[2,128,256]{2,1,0:T(8,128)(2,1)} %w_keys.1, ...), custom_call_target="tpu_custom_call" | custom-call | tf_op jit(solution)/shard_map/pallas_call | solution.py:476
  33.9 1.7 %copy.16 = bf16[2,256,256]{2,1,0:T(8,128)(2,1)} copy(bf16[2,256,256]{2,1,0:T(8,128)(2,1)} %bitcast.3) | data formatting | bytes 524288

commit v2 on v1

--- a/solution.py
+++ b/solution.py
@@ -11,6 +11,7 @@
 N = 128
 BLOCK = 256
 ROWS_DEV = 8
+VMEM_GRANT = 16 << 20
 
 
 def block_terms(values, keys_in, queries, log_decay, block_len):
@@ -240,40 +241,15 @@
     return normed, update
 
 
-def fused_kernel(
-    parts,
-    heads,
-    values,
-    keys_in,
-    queries,
-    steps,
-    w_values,
-    w_keys,
-    w_step,
-    gain_first,
-    gain_second,
-    rates_first,
-    skip_first,
-    step_bias,
-    rates_second,
-    skip_second,
-    out,
-    v_buf,
-    k_buf,
-    q_buf,
-    step_buf,
-    wv_buf,
-    wk_buf,
-    first_buf,
-    turn_buf,
-    send_buf,
-    own_sem,
-    in_send,
-    in_recv,
-    out_own,
-    out_send,
-    out_recv,
-):
+def fused_kernel(parts, heads, *refs):
+    values, keys_in, queries, steps, w_values, w_keys = refs[:6]
+    small_in, out = refs[6:14], refs[14]
+    v_buf, k_buf, q_buf, step_buf, wv_buf, wk_buf = refs[15:21]
+    small = refs[21:29]
+    w_step, gain_first, gain_second = small[:3]
+    rates_first, skip_first, step_bias, rates_second, skip_second = small[3:]
+    first_buf, turn_buf, send_buf = refs[29:32]
+    own_sem, in_send, in_recv, out_own, out_send, out_recv = refs[32:]
     me = lax.axis_index("seq")
     length, width = v_buf.shape[1:]
     rows_all, cols_here = send_buf.shape[1:3]
@@ -293,6 +269,10 @@
         )
 
     landing = (step_buf, k_buf, q_buf, v_buf)
+    turn = jnp.where(me < parts // 2, parts - 1, 1)
+
+    def peer(hop):
+        return lax.rem(me + turn * hop, parts)
 
     barrier = pltpu.get_barrier_semaphore()
     for hop in range(1, parts):
@@ -308,13 +288,15 @@
     ]
     own.append(pltpu.make_async_copy(w_values.at[my_head], wv_buf, own_sem.at[len(landing)]))
     own.append(pltpu.make_async_copy(w_keys.at[my_head], wk_buf, own_sem.at[len(landing) + 1]))
+    for index, (src, dst) in enumerate(zip(small_in, small)):
+        own.append(pltpu.make_async_copy(src, dst, own_sem.at[len(landing) + 2 + index]))
     for copy in own:
         copy.start()
     pl.semaphore_wait(barrier, parts - 1)
 
     sends = []
     for hop in range(1, parts):
-        target = lax.rem(me + hop, parts)
+        target = peer(hop)
         for kind, (src, dst) in enumerate(zip(pieces(target), landing)):
             copy = pltpu.make_async_remote_copy(
                 src_ref=src,
@@ -346,6 +328,9 @@
         0.0,
     ).astype(jnp.bfloat16)
 
+    for copy in own:
+        copy.wait()
+
     def pick(ref, axis_size, select):
         chosen = select(0)
         for head in range(1, axis_size):
@@ -357,9 +342,6 @@
     step_row = pick(w_step, heads, lambda h: w_step[...].astype(jnp.float32)[h : h + 1, :])
     step_rows = jnp.broadcast_to(step_row, (16, width)).astype(jnp.bfloat16)
     skip_one, skip_two = skip_first[my_head], skip_second[my_head]
-
-    for copy in own:
-        copy.wait()
 
     state = None
     for block in range(parts):
@@ -413,7 +395,7 @@
             return out.at[slab, :, pl.ds(block * cols_here, cols_here), lanes(head)]
 
         for hop in range(1, parts):
-            target = lax.rem(me + hop, parts)
+            target = peer(hop)
             copy = pltpu.make_async_remote_copy(
                 src_ref=home(target),
                 dst_ref=place(me),
@@ -470,16 +452,14 @@
     grid_side = math.isqrt(parts * length)
     rows_here, cols_here = grid_side // parts, length // grid_side
     anywhere = pl.BlockSpec(memory_space=pl.ANY)
-    vmem = pl.BlockSpec(memory_space=pltpu.VMEM)
-    smem = pl.BlockSpec(memory_space=pltpu.SMEM)
     dma = pltpu.SemaphoreType.DMA
     mixed = pl.pallas_call(
         functools.partial(fused_kernel, parts, heads),
         out_shape=jax.ShapeDtypeStruct(
             (slab_count, rows_here, grid_side, feat_width), jnp.bfloat16
         ),
-        in_specs=[anywhere] * 6 + [vmem] * 3 + [smem] * 5,
-        out_specs=anywhere,
+        in_specs=[anywhere] * 14,
+        out_specs=pl.BlockSpec(memory_space=pltpu.VMEM),
         scratch_shapes=[
             pltpu.VMEM((parts, length, width), jnp.bfloat16),
             pltpu.VMEM((parts, length, width), jnp.bfloat16),
@@ -487,32 +467,45 @@
             pltpu.VMEM((parts, heads, length), jnp.float32),
             pltpu.VMEM(w_values.shape[1:], jnp.bfloat16),
             pltpu.VMEM(w_keys.shape[1:], jnp.bfloat16),
+            pltpu.VMEM(w_step.shape, jnp.bfloat16),
+            pltpu.VMEM((1, feat_width), jnp.float32),
+            pltpu.VMEM((1, feat_width), jnp.float32),
+        ]
+        + [pltpu.SMEM((heads,), jnp.float32)] * 5
+        + [
             pltpu.VMEM((parts * length, width), jnp.float32),
             pltpu.VMEM((parts, length, width), jnp.float32),
             pltpu.VMEM((parts, grid_side, cols_here, width), jnp.bfloat16),
-            dma((6,)),
+            dma((14,)),
             dma((4, parts)),
             dma((4, parts)),
             dma((parts,)),
             dma((parts, parts)),
             dma((parts, parts)),
         ],
-        compiler_params=pltpu.CompilerParams(collective_id=0, has_side_effects=True),
+        compiler_params=pltpu.CompilerParams(
+            collective_id=0, has_side_effects=True, vmem_limit_bytes=VMEM_GRANT
+        ),
     )(
-        values_first,
-        keys_first,
-        queries_first,
-        steps_first,
-        w_values,
-        w_keys,
-        w_step,
-        gain_first.reshape(1, -1),
-        gain_second.reshape(1, -1),
-        rates_first,
-        skip_first,
-        step_bias,
-        rates_second,
-        skip_second,
+        *(
+            pltpu.with_memory_space_constraint(array, pltpu.HBM)
+            for array in (
+                values_first,
+                keys_first,
+                queries_first,
+                steps_first,
+                w_values,
+                w_keys,
+                w_step,
+                gain_first.reshape(1, -1),
+                gain_second.reshape(1, -1),
+                rates_first,
+                skip_first,
+                step_bias,
+                rates_second,
+                skip_second,
+            )
+        )
     )
     return mixed.reshape(values_first.shape)
 

time: 35.8 us -> 33.3 us (0.930)
  Pallas kernels: 33.9 us -> 32.5 us
  local copies, waits for them, and re-layouts: 1.67 us -> 0.71 us
    pallas_call x1, Pallas kernels: 33.9 us -> 32.5 us  [local_fused(): pl.pallas_call(functools.partial(fused_kernel, parts, heads), out_shape=j...]
    unnamed x1, local copies, waits for them, and re-layouts: 1.67 us -> 0.71 us
where the time goes in v2:
time: 33.3 us; the launch traced here: 33.2 us
  Pallas kernels  32.5 us (98%)
  local copies, waits for them, and re-layouts  0.71 us (2%)
    pallas_call x1, Pallas kernels, local_fused(): pl.pallas_call(functools.partial(fused_kernel, parts, heads), out_shape=j...  32.5 us
    unnamed x1, local copies, waits for them, and re-layouts  0.71 us

profile of v2, /device:TPU:0, one launch (start us, length us, event | category | flops | bytes accessed | tf_op | source)
XLA Modules:
  0.0 33.2 jit_solution(14808337546846695756)
XLA Ops:
  0.0 32.5 %shard_map.136 = bf16[2,8,32,256]{3,2,1,0:T(8,128)(2,1)S(1)} custom-call(bf16[2,256,256]{2,1,0:T(8,128)(2,1)} %refs_0_.1, bf16[2,256,256]{2,1,0:T(8,128)(2,1)} %refs_1_.1, bf16[2,256,256]{2,1,0:T(8,128)(2,1)} %refs_2_.1, f32[2,2,256]{2,1,0:T(2,128)} %refs_3_.1, bf16[2,128,128]{2,1,0:T(8,128)(2,1)} %refs_4_.1, bf16[2,128,256]{2,1,0:T(8,128)(2,1)} %refs_5_.1, ...), custom_call_target="tpu_custom_call" | custom-call | tf_op jit(solution)/shard_map/pallas_call | solution.py:456
  32.5 0.7 %copy.16 = bf16[2,256,256]{2,1,0:T(8,128)(2,1)} copy(bf16[2,256,256]{2,1,0:T(8,128)(2,1)S(1)} %bitcast.3) | data formatting | bytes 524288

commit v3 on v2

--- a/solution.py
+++ b/solution.py
@@ -195,10 +195,13 @@
     )
 
 
-def scan_block(values, keys_in, queries, run_row, state, skip, gain):
+def column_of(run_row, width):
+    return jnp.transpose(jnp.broadcast_to(run_row, (width, run_row.shape[1])))
+
+
+def inner_part(values, keys_in, queries, run_row, run_col, skip):
     length, width = values.shape
     half = length // 2
-    run_col = jnp.transpose(jnp.broadcast_to(run_row, (width, length)))
     lower = lax.broadcasted_iota(jnp.int32, (half, half), 0) >= lax.broadcasted_iota(
         jnp.int32, (half, half), 1
     )
@@ -227,18 +230,26 @@
         ],
         axis=0,
     )
-    raw = inner + skip * values.astype(jnp.float32)
-    if state is not None:
-        outer = jnp.dot(queries, state.astype(jnp.bfloat16), preferred_element_type=jnp.float32)
-        raw = raw + jnp.exp(run_col) * outer
-    mean_sq = jnp.mean(raw * raw, axis=1, keepdims=True)
-    normed = (raw * lax.rsqrt(mean_sq + 1e-05) * gain).astype(jnp.bfloat16)
-    last = run_col[length - 1 : length, :]
+    return inner + skip * values.astype(jnp.float32)
+
+
+def state_part(values, keys_in, run_col):
+    last = run_col[run_col.shape[0] - 1 :, :]
     weighted = (keys_in.astype(jnp.float32) * jnp.exp(last - run_col)).astype(jnp.bfloat16)
-    update = dot_tn(weighted, values)
-    if state is not None:
-        update = update + jnp.exp(last) * state
-    return normed, update
+    return dot_tn(weighted, values)
+
+
+def outer_part(queries, run_col, state):
+    outer = jnp.dot(queries, state.astype(jnp.bfloat16), preferred_element_type=jnp.float32)
+    return jnp.exp(run_col) * outer
+
+
+def advanced(state, run_col, update):
+    return jnp.exp(run_col[run_col.shape[0] - 1 :, :]) * state + update
+
+
+def norm_factor(raw):
+    return lax.rsqrt(jnp.mean(raw * raw, axis=1, keepdims=True) + 1e-05)
 
 
 def fused_kernel(parts, heads, *refs):
@@ -248,78 +259,77 @@
     small = refs[21:29]
     w_step, gain_first, gain_second = small[:3]
     rates_first, skip_first, step_bias, rates_second, skip_second = small[3:]
-    first_buf, turn_buf, send_buf = refs[29:32]
-    own_sem, in_send, in_recv, out_own, out_send, out_recv = refs[32:]
+    stage_raw, stage_state, raw_buf, state_buf, out_maps, out_steps = refs[29:35]
+    first_buf, turn_buf, send_buf = refs[35:38]
+    own_sem, unit_sem, in_send, in_recv, out_own, out_send, out_recv = refs[38:]
     me = lax.axis_index("seq")
     length, width = v_buf.shape[1:]
     rows_all, cols_here = send_buf.shape[1:3]
     rows_here = rows_all // parts
     my_slab, my_head = me // heads, lax.rem(me, heads)
+    turn = jnp.where(me < parts // 2, parts - 1, 1)
+
+    def peer(hop):
+        return lax.rem(me + turn * hop, parts)
 
     def lanes(head):
         return pl.ds(pl.multiple_of(head * width, width), width)
 
-    def pieces(owner):
-        slab, head = owner // heads, lax.rem(owner, heads)
-        return (
-            steps.at[slab],
-            keys_in.at[slab, :, lanes(head)],
-            queries.at[slab, :, lanes(head)],
-            values.at[slab, :, lanes(head)],
-        )
-
-    landing = (step_buf, k_buf, q_buf, v_buf)
-    turn = jnp.where(me < parts // 2, parts - 1, 1)
-
-    def peer(hop):
-        return lax.rem(me + turn * hop, parts)
+    def unit_of(array, unit):
+        return array.at[unit // heads, :, lanes(lax.rem(unit, heads))]
 
     barrier = pltpu.get_barrier_semaphore()
     for hop in range(1, parts):
         pl.semaphore_signal(
             barrier,
             inc=1,
-            device_id={"seq": lax.rem(me + hop, parts)},
+            device_id={"seq": peer(hop)},
             device_id_type=pl.DeviceIdType.MESH,
         )
     own = [
-        pltpu.make_async_copy(src, dst.at[me], own_sem.at[kind])
-        for kind, (src, dst) in enumerate(zip(pieces(me), landing))
+        pltpu.make_async_copy(steps, step_buf, own_sem.at[0]),
+        pltpu.make_async_copy(w_values.at[my_head], wv_buf, own_sem.at[1]),
+        pltpu.make_async_copy(w_keys.at[my_head], wk_buf, own_sem.at[2]),
     ]
-    own.append(pltpu.make_async_copy(w_values.at[my_head], wv_buf, own_sem.at[len(landing)]))
-    own.append(pltpu.make_async_copy(w_keys.at[my_head], wk_buf, own_sem.at[len(landing) + 1]))
     for index, (src, dst) in enumerate(zip(small_in, small)):
-        own.append(pltpu.make_async_copy(src, dst, own_sem.at[len(landing) + 2 + index]))
+        own.append(pltpu.make_async_copy(src, dst, own_sem.at[3 + index]))
+    for unit in range(parts):
+        for kind, (src, dst) in enumerate(((keys_in, k_buf), (queries, q_buf), (values, v_buf))):
+            own.append(
+                pltpu.make_async_copy(unit_of(src, unit), dst.at[unit], unit_sem.at[kind, unit])
+            )
     for copy in own:
         copy.start()
     pl.semaphore_wait(barrier, parts - 1)
 
-    sends = []
-    for hop in range(1, parts):
-        target = peer(hop)
-        for kind, (src, dst) in enumerate(zip(pieces(target), landing)):
-            copy = pltpu.make_async_remote_copy(
-                src_ref=src,
-                dst_ref=dst.at[me],
-                send_sem=in_send.at[kind, hop],
-                recv_sem=in_recv.at[kind, me],
-                device_id={"seq": target},
-                device_id_type=pl.DeviceIdType.MESH,
-            )
-            copy.start()
-            sends.append(copy)
-
-    def await_block(source, kinds):
-        for kind in kinds:
-            src, dst = pieces(me)[kind], landing[kind]
-            pltpu.make_async_remote_copy(
-                src_ref=src,
-                dst_ref=dst.at[source],
-                send_sem=in_send.at[kind, 0],
-                recv_sem=in_recv.at[kind, source],
-                device_id={"seq": source},
-                device_id_type=pl.DeviceIdType.MESH,
-            ).wait_recv()
+    def remote(kind, hop, src, dst, target, slot):
+        return pltpu.make_async_remote_copy(
+            src_ref=src,
+            dst_ref=dst,
+            send_sem=in_send.at[kind, hop],
+            recv_sem=in_recv.at[kind, slot],
+            device_id={"seq": target},
+            device_id_type=pl.DeviceIdType.MESH,
+        )
+
+    def steps_copy(hop, target):
+        src = steps.at[target // heads]
+        return remote(0, hop, src, out_steps.at[me], target, me)
+
+    def maps_copy(hop, target):
+        return remote(1, hop, unit_of(queries, target), out_maps.at[me], target, me)
+
+    def state_copy(hop, target):
+        return remote(2, hop, stage_state.at[hop], state_buf.at[me], target, me)
+
+    def raw_copy(hop, target):
+        return remote(3, hop, stage_raw.at[hop], raw_buf.at[me], target, me)
+
+    @pl.when(me > 0)
+    def _():
+        for hop in range(1, parts):
+            steps_copy(hop, peer(hop)).start()
+            maps_copy(hop, peer(hop)).start()
 
     upper = jnp.where(
         lax.broadcasted_iota(jnp.int32, (length, length), 0)
@@ -331,31 +341,78 @@
     for copy in own:
         copy.wait()
 
-    def pick(ref, axis_size, select):
+    def pick(head, select):
         chosen = select(0)
-        for head in range(1, axis_size):
-            chosen = jnp.where(my_head == head, select(head), chosen)
+        for index in range(1, heads):
+            chosen = jnp.where(head == index, select(index), chosen)
         return chosen
 
-    gain_one = pick(gain_first, heads, lambda h: gain_first[:, h * width : (h + 1) * width])
-    gain_two = pick(gain_second, heads, lambda h: gain_second[:, h * width : (h + 1) * width])
-    step_row = pick(w_step, heads, lambda h: w_step[...].astype(jnp.float32)[h : h + 1, :])
+    def gain_of(gain, head):
+        return pick(head, lambda h: gain[:, h * width : (h + 1) * width])
+
+    step_row = pick(my_head, lambda h: w_step[...].astype(jnp.float32)[h : h + 1, :])
     step_rows = jnp.broadcast_to(step_row, (16, width)).astype(jnp.bfloat16)
-    skip_one, skip_two = skip_first[my_head], skip_second[my_head]
+    gain_one, gain_two = gain_of(gain_first, my_head), gain_of(gain_second, my_head)
+    skip_two = skip_second[my_head]
+
+    def row_of(step_rows_one, rate):
+        return cumsum_rows(jnp.broadcast_to(-rate * step_rows_one, (8, length)), upper)[0:1]
+
+    for hop in (*range(1, parts), 0):
+        unit = peer(hop)
+        head = lax.rem(unit, heads)
+        run_row = row_of(step_buf[unit // heads, pl.ds(head, 1), :], rates_first[head])
+        run_col = column_of(run_row, width)
+        values_one, keys_one, queries_one = v_buf[unit], k_buf[unit], q_buf[unit]
+        update = state_part(values_one, keys_one, run_col).astype(jnp.bfloat16)
+        if hop:
+            stage_state[hop] = update
+
+            @pl.when(me < parts - 1)
+            def _():
+                state_copy(hop, unit).start()
+        else:
+            state_buf[me] = update
+        raw = inner_part(values_one, keys_one, queries_one, run_row, run_col, skip_first[head])
+        scale = norm_factor(raw) * gain_of(gain_first, head)
+        sent = (raw * jnp.where(me == 0, scale, 1.0)).astype(jnp.bfloat16)
+        if hop:
+            stage_raw[hop] = sent
+            raw_copy(hop, unit).start()
+        else:
+            raw_buf[me] = sent
+
+    def await_from(block, kind, src, dst):
+        @pl.when(me != block)
+        def _():
+            remote(kind, 0, src, dst.at[block], block, block).wait_recv()
 
     state = None
     for block in range(parts):
-        @pl.when(me != block)
-        def _():
-            await_block(block, range(len(landing)))
-
-        log_row = -rates_first[my_head] * step_buf[block, pl.ds(my_head, 1), :]
-        run_row = cumsum_rows(jnp.broadcast_to(log_row, (8, length)), upper)[0:1]
-        normed, state = scan_block(
-            v_buf[block], k_buf[block], q_buf[block], run_row, state, skip_one, gain_one
-        )
-        first_buf[pl.ds(block * length, length), :] = normed.astype(jnp.float32)
-
+        if block:
+            await_from(block, 0, steps.at[0], out_steps)
+            await_from(block, 1, q_buf.at[0], out_maps)
+            mine = me == block
+            step_one = jnp.where(
+                mine,
+                step_buf[my_slab, pl.ds(my_head, 1), :],
+                out_steps[block, pl.ds(my_head, 1), :],
+            )
+            run_col = column_of(row_of(step_one, rates_first[my_head]), width)
+            maps_one = jnp.where(mine, q_buf[me], out_maps[block])
+            raw_add = outer_part(maps_one, run_col, state)
+        await_from(block, 3, stage_raw.at[0], raw_buf)
+        raw = raw_buf[block].astype(jnp.float32)
+        if block:
+            raw = raw + raw_add
+            raw = (raw * norm_factor(raw) * gain_one).astype(jnp.bfloat16).astype(jnp.float32)
+        first_buf[pl.ds(block * length, length), :] = raw
+        if block < parts - 1:
+            await_from(block, 2, stage_state.at[0], state_buf)
+            update = state_buf[block].astype(jnp.float32)
+            state = advanced(state, run_col, update) if block else update
+
+    sends = []
     state = None
     for block in range(parts):
         columns = jnp.concatenate(
@@ -375,10 +432,16 @@
         shifted = pre + step_bias[my_head]
         soft = jnp.maximum(shifted, 0.0) + jnp.log1p(jnp.exp(-jnp.abs(shifted)))
         run_row = cumsum_rows(-rates_second[my_head] * soft, upper)[0:1]
+        run_col = column_of(run_row, width)
         half = keys_two.shape[1] // 2
-        normed, state = scan_block(
-            values_two, keys_two[:, :half], keys_two[:, half:], run_row, state, skip_two, gain_two
-        )
+        keys_now, queries_now = keys_two[:, :half], keys_two[:, half:]
+        raw = inner_part(values_two, keys_now, queries_now, run_row, run_col, skip_two)
+        if block:
+            raw = raw + outer_part(queries_now, run_col, state)
+        if block < parts - 1:
+            update = state_part(values_two, keys_now, run_col)
+            state = advanced(state, run_col, update) if block else update
+        normed = (raw * norm_factor(raw) * gain_two).astype(jnp.bfloat16)
         turn_buf[block] = normed.astype(jnp.float32)
         for row in range(rows_all):
             total = (
@@ -427,6 +490,19 @@
             ).wait_recv()
     for copy in sends:
         copy.wait_send()
+    for hop in range(1, parts):
+        raw_copy(hop, peer(hop)).wait_send()
+
+    @pl.when(me > 0)
+    def _():
+        for hop in range(1, parts):
+            steps_copy(hop, peer(hop)).wait_send()
+            maps_copy(hop, peer(hop)).wait_send()
+
+    @pl.when(me < parts - 1)
+    def _():
+        for hop in range(1, parts):
+            state_copy(hop, peer(hop)).wait_send()
 
 
 def local_fused(
@@ -464,7 +540,7 @@
             pltpu.VMEM((parts, length, width), jnp.bfloat16),
             pltpu.VMEM((parts, length, width), jnp.bfloat16),
             pltpu.VMEM((parts, length, width), jnp.bfloat16),
-            pltpu.VMEM((parts, heads, length), jnp.float32),
+            pltpu.VMEM(steps_first.shape, jnp.float32),
             pltpu.VMEM(w_values.shape[1:], jnp.bfloat16),
             pltpu.VMEM(w_keys.shape[1:], jnp.bfloat16),
             pltpu.VMEM(w_step.shape, jnp.bfloat16),
@@ -473,10 +549,17 @@
         ]
         + [pltpu.SMEM((heads,), jnp.float32)] * 5
         + [
+            pltpu.VMEM((parts, length, width), jnp.bfloat16),
+            pltpu.VMEM((parts, width, width), jnp.bfloat16),
+            pltpu.VMEM((parts, length, width), jnp.bfloat16),
+            pltpu.VMEM((parts, width, width), jnp.bfloat16),
+            pltpu.VMEM((parts, length, width), jnp.bfloat16),
+            pltpu.VMEM((parts, heads, length), jnp.float32),
             pltpu.VMEM((parts * length, width), jnp.float32),
             pltpu.VMEM((parts, length, width), jnp.float32),
             pltpu.VMEM((parts, grid_side, cols_here, width), jnp.bfloat16),
-            dma((14,)),
+            dma((11,)),
+            dma((3, parts)),
             dma((4, parts)),
             dma((4, parts)),
             dma((parts,)),

time: 33.3 us -> 26.9 us (0.81)
  Pallas kernels: 32.5 us -> 26.1 us
    pallas_call x1, Pallas kernels: 32.5 us -> 26.1 us  [local_fused(): pl.pallas_call(functools.partial(fused_kernel, parts, heads), out_shape=j...]
where the time goes in v3:
time: 26.9 us; the launch traced here: 26.8 us
  Pallas kernels  26.1 us (97%)
  local copies, waits for them, and re-layouts  0.71 us (3%)
    pallas_call x1, Pallas kernels, local_fused(): pl.pallas_call(functools.partial(fused_kernel, parts, heads), out_shape=j...  26.1 us
    unnamed x1, local copies, waits for them, and re-layouts  0.71 us

profile of v3, /device:TPU:0, one launch (start us, length us, event | category | flops | bytes accessed | tf_op | source)
XLA Modules:
  0.0 26.8 jit_solution(16299786406746762414)
XLA Ops:
  0.0 26.1 %shard_map.136 = bf16[2,8,32,256]{3,2,1,0:T(8,128)(2,1)S(1)} custom-call(bf16[2,256,256]{2,1,0:T(8,128)(2,1)} %refs_0_.1, bf16[2,256,256]{2,1,0:T(8,128)(2,1)} %refs_1_.1, bf16[2,256,256]{2,1,0:T(8,128)(2,1)} %refs_2_.1, f32[2,2,256]{2,1,0:T(2,128)} %refs_3_.1, bf16[2,128,128]{2,1,0:T(8,128)(2,1)} %refs_4_.1, bf16[2,128,256]{2,1,0:T(8,128)(2,1)} %refs_5_.1, ...), custom_call_target="tpu_custom_call" | custom-call | tf_op jit(solution)/shard_map/pallas_call | solution.py:532
  26.1 0.7 %copy.16 = bf16[2,256,256]{2,1,0:T(8,128)(2,1)} copy(bf16[2,256,256]{2,1,0:T(8,128)(2,1)S(1)} %bitcast.3) | data formatting | bytes 524288

commit v4 on v3

--- a/solution.py
+++ b/solution.py
@@ -328,8 +328,9 @@
     @pl.when(me > 0)
     def _():
         for hop in range(1, parts):
+            maps_copy(hop, peer(hop)).start()
+        for hop in range(1, parts):
             steps_copy(hop, peer(hop)).start()
-            maps_copy(hop, peer(hop)).start()
 
     upper = jnp.where(
         lax.broadcasted_iota(jnp.int32, (length, length), 0)
@@ -365,22 +366,20 @@
         run_col = column_of(run_row, width)
         values_one, keys_one, queries_one = v_buf[unit], k_buf[unit], q_buf[unit]
         update = state_part(values_one, keys_one, run_col).astype(jnp.bfloat16)
-        if hop:
-            stage_state[hop] = update
-
-            @pl.when(me < parts - 1)
-            def _():
-                state_copy(hop, unit).start()
-        else:
-            state_buf[me] = update
         raw = inner_part(values_one, keys_one, queries_one, run_row, run_col, skip_first[head])
         scale = norm_factor(raw) * gain_of(gain_first, head)
         sent = (raw * jnp.where(me == 0, scale, 1.0)).astype(jnp.bfloat16)
         if hop:
             stage_raw[hop] = sent
+            stage_state[hop] = update
             raw_copy(hop, unit).start()
+
+            @pl.when(me < parts - 1)
+            def _():
+                state_copy(hop, unit).start()
         else:
             raw_buf[me] = sent
+            state_buf[me] = update
 
     def await_from(block, kind, src, dst):
         @pl.when(me != block)
@@ -438,9 +437,6 @@
         raw = inner_part(values_two, keys_now, queries_now, run_row, run_col, skip_two)
         if block:
             raw = raw + outer_part(queries_now, run_col, state)
-        if block < parts - 1:
-            update = state_part(values_two, keys_now, run_col)
-            state = advanced(state, run_col, update) if block else update
         normed = (raw * norm_factor(raw) * gain_two).astype(jnp.bfloat16)
         turn_buf[block] = normed.astype(jnp.float32)
         for row in range(rows_all):
@@ -470,6 +466,9 @@
             copy.start()
             sends.append(copy)
         pltpu.make_async_copy(home(me), place(me), out_own.at[block]).start()
+        if block < parts - 1:
+            update = state_part(values_two, keys_now, run_col)
+            state = advanced(state, run_col, update) if block else update
 
     for block in range(parts):
         def place(owner):

time: 26.9 us -> 26.8 us (level)
  no operation moved by 1% of the time
where the time goes in v4:
time: 26.8 us; the launch traced here: 26.6 us
  Pallas kernels  25.9 us (97%)
  local copies, waits for them, and re-layouts  0.71 us (3%)
    pallas_call x1, Pallas kernels, local_fused(): pl.pallas_call(functools.partial(fused_kernel, parts, heads), out_shape=j...  25.9 us
    unnamed x1, local copies, waits for them, and re-layouts  0.71 us

profile of v4, /device:TPU:0, one launch (start us, length us, event | category | flops | bytes accessed | tf_op | source)
XLA Modules:
  0.0 26.6 jit_solution(5894115221148199023)
XLA Ops:
  0.0 25.9 %shard_map.136 = bf16[2,8,32,256]{3,2,1,0:T(8,128)(2,1)S(1)} custom-call(bf16[2,256,256]{2,1,0:T(8,128)(2,1)} %refs_0_.1, bf16[2,256,256]{2,1,0:T(8,128)(2,1)} %refs_1_.1, bf16[2,256,256]{2,1,0:T(8,128)(2,1)} %refs_2_.1, f32[2,2,256]{2,1,0:T(2,128)} %refs_3_.1, bf16[2,128,128]{2,1,0:T(8,128)(2,1)} %refs_4_.1, bf16[2,128,256]{2,1,0:T(8,128)(2,1)} %refs_5_.1, ...), custom_call_target="tpu_custom_call" | custom-call | tf_op jit(solution)/shard_map/pallas_call | solution.py:531
  25.9 0.7 %copy.16 = bf16[2,256,256]{2,1,0:T(8,128)(2,1)} copy(bf16[2,256,256]{2,1,0:T(8,128)(2,1)S(1)} %bitcast.3) | data formatting | bytes 524288
